TPU v7x, 512 devices: a whole 4x8x8 slice. The times are simulated.
512 devices in a mesh: segment: 8 (over x, core), adapter: 64 (over z, y).
Axes of the slice: x: 4, y: 8, z: 8, core: 2. Of those that a mesh axis runs over, the one named last changes fastest.
Arguments:
- incoming: bfloat16 [4096, 8192], P(('segment', 'adapter')), may hold values from -6 to 6
- attention_norm_gain: float32 [8, 8192], P('segment'), may hold values from 0.1 to 1.9
- query_weight: bfloat16 [8, 8192, 8192], P('segment', None, 'adapter'), may hold values from -0.0625 to 0.0625
- adapter_down_weight: bfloat16 [8, 64, 8192, 64], P('segment', 'adapter'), may hold values from -0.0625 to 0.0625
- adapter_up_weight: bfloat16 [8, 64, 64, 8192], P('segment', None, None, 'adapter'), may hold values from -0.75 to 0.75
- request_adapter_index: int32 [4096], P('segment'), may hold values from 0 to 63, as said below
- cache_valid_length: int32 [4096], P('segment'), may hold values from 1 to 16
- key_value_cache: bfloat16 [4096, 2, 16, 1024], P(('segment', 'adapter')), may hold values from -1500 to 1500, as said below
Outputs:
- context: bfloat16 [4096, 8192], P(('segment', 'adapter'))
Inputs may be any that keep to these rules, and one draw needn't show every extreme that they name: `request_adapter_index`: adapter a is owned by index a // 1 of adapter. At most 32 of the 512 requests of one section name adapters of one owner, and in every section some owner has exactly 32. `key_value_cache`: positions at or after a request's length hold unused entries.
All inputs are finite; a program needn't handle non-finite values.
Results may differ from a plain program's by a relative error of at most 0.04.
Values may be sent and summed in bfloat16 or wider, within the bound.
No kernel may reach another device: no remote copies, remote signals or barrier semaphores. Data moves between devices by JAX's collectives and lax.ppermute only.
A program may use at most 64 MiB of HBM per device.

v0:
```python
import jax
import jax.numpy as jnp
from jax import lax
from jax.sharding import PartitionSpec as P

MODEL_WIDTH = 8192
HEADS = 64
KVH = 8
HD = 128
CTX = 16
adapter_scale = 0.5
norm_eps = 1e-05


def from_behind(value, axis, by):
    devices = lax.axis_size(axis)
    return lax.ppermute(value, axis, [(i, (i + by) % devices) for i in range(devices)])


def body(
    incoming,
    attention_norm_gain,
    query_weight,
    adapter_down_weight,
    adapter_up_weight,
    request_adapter_index,
    cache_valid_length,
    key_value_cache,
):
    received_rows = from_behind(incoming, "segment", 1)
    values = received_rows.astype(jnp.float32)
    mean_square = jnp.mean(values * values, axis=-1, keepdims=True)
    normalized_input = (values * lax.rsqrt(mean_square + norm_eps) * attention_norm_gain[0]).astype(
        jnp.bfloat16
    )
    tok_dev = received_rows.shape[0]
    position = lax.axis_index("adapter")
    segment_rows = request_adapter_index.shape[0]
    weight = query_weight[0]
    column_list = weight.shape[1]
    down_matrices = adapter_down_weight[0]
    ad_dev = down_matrices.shape[0]
    adapter_rank_width = down_matrices.shape[2]
    adapter_bank = adapter_up_weight.shape[1]
    owner_of = request_adapter_index // ad_dev
    local_of = request_adapter_index % ad_dev
    row_piece = lax.all_gather(normalized_input, "adapter", axis=0, tiled=True)
    plain = jnp.dot(row_piece, weight, preferred_element_type=jnp.float32)
    shrunk = jnp.einsum("td,adr->tar", row_piece, down_matrices, preferred_element_type=jnp.float32)
    projected = jnp.concatenate(
        [plain, shrunk.reshape(row_piece.shape[0], ad_dev * adapter_rank_width)], axis=1
    )
    base_query = projected[:, :column_list]
    shrunk_all = projected[:, column_list:].reshape(segment_rows, ad_dev, adapter_rank_width)
    select_mask = (local_of[:, None] == jnp.arange(ad_dev, dtype=jnp.int32)[None, :]) & (
        owner_of == position
    )[:, None]
    shrunk_mine = jnp.sum(shrunk_all * select_mask[:, :, None].astype(jnp.float32), axis=1)
    shrunk_tok = lax.psum(shrunk_mine, "adapter").astype(jnp.bfloat16)
    adapter_hot = (
        request_adapter_index[:, None] == jnp.arange(adapter_bank, dtype=jnp.int32)[None, :]
    ).astype(jnp.bfloat16)
    spread = (adapter_hot[:, :, None] * shrunk_tok[:, None, :]).reshape(
        segment_rows, adapter_bank * adapter_rank_width
    )
    adapter_update = jnp.dot(
        spread,
        adapter_up_weight[0].reshape(adapter_bank * adapter_rank_width, column_list),
        preferred_element_type=jnp.float32,
    )
    query_rows = (base_query + adapter_scale * adapter_update).astype(jnp.bfloat16)
    own_queries = lax.all_to_all(query_rows, "adapter", split_axis=0, concat_axis=1, tiled=True)
    own_lengths = lax.dynamic_slice_in_dim(cache_valid_length, position * tok_dev, tok_dev)
    group_size = HEADS // KVH
    query_heads = own_queries.reshape(tok_dev, KVH, group_size, HD)
    cached_keys = key_value_cache[:, 0].reshape(tok_dev, CTX, KVH, HD)
    cached_values = key_value_cache[:, 1].reshape(tok_dev, CTX, KVH, HD)
    scores = jnp.einsum(
        "tkgd,tckd->tkgc", query_heads, cached_keys, preferred_element_type=jnp.float32
    ) * HD ** (-0.5)
    is_live = jnp.arange(CTX, dtype=jnp.int32)[None, :] < own_lengths[:, None]
    scores = jnp.where(is_live[:, None, None, :], scores, -jnp.inf)
    row_max = jnp.max(scores, axis=-1, keepdims=True)
    expsum = jnp.exp(scores - row_max)
    probs = (expsum / jnp.sum(expsum, axis=-1, keepdims=True)).astype(jnp.bfloat16)
    context = jnp.einsum(
        "tkgc,tckd->tkgd", probs, cached_values, preferred_element_type=jnp.float32
    )
    return context.astype(jnp.bfloat16).reshape(tok_dev, MODEL_WIDTH)


def solution(mesh):
    in_specs = (
        P(("segment", "adapter"), None),
        P("segment", None),
        P("segment", None, "adapter"),
        P("segment", "adapter", None, None),
        P("segment", None, None, "adapter"),
        P("segment"),
        P("segment"),
        P(("segment", "adapter"), None, None, None),
    )
    out_specs = P(("segment", "adapter"), None)
    return jax.shard_map(body, mesh=mesh, in_specs=in_specs, out_specs=out_specs, check_vma=False)
```

profile of v0, /device:TPU:2, one launch (start us, length us, event | category | flops | bytes accessed | tf_op | source)
XLA Modules:
  0.0 437.0 jit_solution(6237502555371092495)
XLA Ops:
  6.5 0.0 copy-start
  6.5 0.0 all-gather.2.cloned.1.call-start
  6.5 0.0 collective-permute-start
  6.5 4.6 %collective-permute-done = bf16[8,8192]{1,0:T(8,128)(2,1)S(1)} collective-permute-done((bf16[8,8192]{1,0:T(8,128)(2,1)}, bf16[8,8192]{1,0:T(8,128)(2,1)S(1)}, u32[]{:S(2)}, u32[]{:S(2)}) %collective-permute-start) | collective-permute-done | bytes 131104 | tf_op jit(solution)/shard_map/ppermute | solution.py:17
  11.1 0.2 fusion.11
  11.3 1.5 fusion.13
  12.8 0.0 all-gather.2.cloned.1.call-update
  12.9 0.7 compare_convert_fusion
  13.6 0.7 fusion.19
  14.3 102.8 %all-gather.2.cloned.1.call-done = bf16[512,8192]{1,0:T(8,128)(2,1)} async-done(((bf16[8,8192]{1,0:T(8,128)(2,1)}), bf16[512,8192]{1,0:T(8,128)(2,1)}) %all-gather.2.cloned.1.call-update) | async-done | bytes 8388624 | tf_op jit(solution)/shard_map/all_gather | solution.py:47
  117.0 6.3 %convolution_multiply_fusion.2 = f32[512,64]{0,1:T(8,128)S(1)} fusion(bf16[512,8192]{1,0:T(8,128)(2,1)} %all-gather.2.cloned.1.call-done, bf16[1,1,8192,64]{2,3,1,0:T(8,128)(2,1)} %param.11, f32[512]{0:T(512)S(1)} %compare_convert_fusion), kind=kOutput, calls=%fused_computation.14 | convolution fusion | flops 536903680 | bytes 9570304 | tf_op jit(solution)/shard_map/td,adr->tar/dot_general | solution.py:49
  123.3 277.7 %all-reduce.1 = bf16[512,64]{0,1:T(8,128)(2,1)S(1)} all-reduce(f32[512,64]{0,1:T(8,128)S(1)} %convolution_multiply_fusion.2), channel_id=1, replica_groups=mesh['segment'=8,'adapter'=64] {'adapter'}, use_global_device_ids=true, to_apply=%region_1.2 | all-reduce | flops 32768 | bytes 196608 | tf_op jit(solution)/shard_map/psum | solution.py:59
  401.0 0.3 broadcast_multiply_fusion
  401.3 0.0 copy-done
  401.3 0.0 copy-start.1
  401.3 5.8 %fusion.1 = f32[512,128]{1,0:T(8,128)S(1)} fusion(bf16[512,8192]{1,0:T(8,128)(2,1)} %all-gather.2.cloned.1.call-done, bf16[1,8192,128]{2,1,0:T(8,128)(2,1)S(1)} %copy-done), kind=kOutput, calls=%fused_computation.1 | convolution fusion | flops 1073741824 | bytes 10747904 | tf_op jit(solution)/shard_map/dot_general | solution.py:48
  407.1 0.0 copy-start.2
  407.1 0.0 copy-done.1
  407.1 2.0 fusion.9
  409.1 6.2 %all-to-all-start = ((bf16[64,8,128]{2,1,0:T(8,128)(2,1)}), bf16[64,8,128]{2,1,0:T(8,128)(2,1)S(1)}, u32[]{:S(2)}, u32[]{:S(2)}) async-start(bf16[64,8,128]{2,1,0:T(8,128)(2,1)} %fusion.9), calls=%async_computation | async-start | bytes 262144 | tf_op jit(solution)/shard_map/all_to_all | solution.py:72
  415.3 0.0 copy-done.2
  415.5 0.8 dynamic_slice.3
  416.2 0.1 iota_compare_fusion.1
  416.3 11.7 %all-to-all-done = bf16[64,8,128]{2,1,0:T(8,128)(2,1)S(1)} async-done(((bf16[64,8,128]{2,1,0:T(8,128)(2,1)}), bf16[64,8,128]{2,1,0:T(8,128)(2,1)S(1)}, u32[]{:S(2)}, u32[]{:S(2)}) %all-to-all-start) | async-done | bytes 131104 | tf_op jit(solution)/shard_map/all_to_all | solution.py:72
  428.0 0.3 fusion.4
  428.2 0.2 fusion.21
  428.5 1.0 fusion.8
  429.5 0.7 copy.26
  (4 shorter events, 0.1 us)
Async XLA Ops:
  6.5 394.7 %copy-start = (bf16[1,8192,128]{2,1,0:T(8,128)(2,1)S(1)}, bf16[1,8192,128]{2,1,0:T(8,128)(2,1)}, u32[]{:S(2)}) copy-start(bf16[1,8192,128]{2,1,0:T(8,128)(2,1)} %param.10) | copy-start | bytes 6291460
  6.5 110.5 %all-gather.2.cloned.1.call-start = ((), (), s32[]{:S(2)}) async-start(), calls=%async_computation.1 | async-start | bytes 8519680 | tf_op jit(solution)/shard_map/all_gather | solution.py:47
  6.5 4.6 %collective-permute-start = (bf16[8,8192]{1,0:T(8,128)(2,1)}, bf16[8,8192]{1,0:T(8,128)(2,1)S(1)}, u32[]{:S(2)}, u32[]{:S(2)}) collective-permute-start(bf16[8,8192]{1,0:T(8,128)(2,1)} %param.8), channel_id=1, source_target_pairs={{0,64},{64,128},{128,192},{192,256},{256,320},{320,384},{384,448},... | collective-permute-start | bytes 393224 | tf_op jit(solution)/shard_map/ppermute | solution.py:17
  401.3 5.8 %copy-start.1 = (bf16[1,64,64,128]{3,2,1,0:T(8,128)(2,1)S(1)}, bf16[1,64,64,128]{3,2,1,0:T(8,128)(2,1)}, u32[]{:S(2)}) copy-start(bf16[1,64,64,128]{3,2,1,0:T(8,128)(2,1)} %param.12) | copy-start | bytes 3145732
  407.1 8.2 %copy-start.2 = (bf16[8,2,16,1024]{3,2,1,0:T(8,128)(2,1)S(1)}, bf16[8,2,16,1024]{3,2,1,0:T(8,128)(2,1)}, u32[]{:S(2)}) copy-start(bf16[8,2,16,1024]{3,2,1,0:T(8,128)(2,1)} %param.15) | copy-start | bytes 1572868
  409.1 18.9 %all-to-all-start = ((bf16[64,8,128]{2,1,0:T(8,128)(2,1)}), bf16[64,8,128]{2,1,0:T(8,128)(2,1)S(1)}, u32[]{:S(2)}, u32[]{:S(2)}) async-start(bf16[64,8,128]{2,1,0:T(8,128)(2,1)} %fusion.9), calls=%async_computation | async-start | bytes 262144 | tf_op jit(solution)/shard_map/all_to_all | solution.py:72
Sparse Core Ops, SparseCore 0:
  13.0 103.9 all-gather.1
where the time goes:
time: 437 us
  blocking collectives  278 us (64%)
  waiting for transfers between devices  119 us (27%)
  matrix products  15.3 us (4%)
  between operations  13.5 us (3%)
  starting transfers between devices  6.2 us (1%)
    psum x1, blocking collectives, body(): shrunk_tok = lax.psum(shrunk_mine, 'adapter').astype(jnp.bfloat16)  278 us
    all_gather x1, waiting for transfers between devices, body(): row_piece = lax.all_gather(normalized_input, 'adapter', axis=0, tiled=True)  103 us
    all_to_all x1, waiting for transfers between devices, body(): lax.all_to_all(query_rows, 'adapter', split_axis=0, concat_axis=1, tiled=...  11.7 us
  transfers between devices with their start and end apart: 3, of which 3 were waited for; matrix products, arithmetic and copies ran while one was open for 1% of the time, Pallas kernels for 0%

commit v1 on v0

--- a/solution.py
+++ b/solution.py
@@ -44,7 +44,11 @@
     adapter_bank = adapter_up_weight.shape[1]
     owner_of = request_adapter_index // ad_dev
     local_of = request_adapter_index % ad_dev
-    row_piece = lax.all_gather(normalized_input, "adapter", axis=0, tiled=True)
+    size = lax.axis_size("adapter")
+    repeats = [size if d == 0 else 1 for d in range(normalized_input.ndim)]
+    row_piece = lax.all_to_all(
+        jnp.tile(normalized_input, repeats), "adapter", split_axis=0, concat_axis=0, tiled=True
+    )
     plain = jnp.dot(row_piece, weight, preferred_element_type=jnp.float32)
     shrunk = jnp.einsum("td,adr->tar", row_piece, down_matrices, preferred_element_type=jnp.float32)
     projected = jnp.concatenate(

time: 437 us -> 622 us (1.42)
  the two profiles are of different devices: /device:TPU:2 before, /device:TPU:6 now
where the time goes in v1:
time: 622 us
  blocking collectives  326 us (52%)
  waiting for transfers between devices  249 us (40%)
  starting transfers between devices  23.8 us (4%)
  matrix products  15 us (2%)
    psum x1, blocking collectives, body(): shrunk_tok = lax.psum(shrunk_mine, 'adapter').astype(jnp.bfloat16)  326 us
    all_to_all x1, waiting for transfers between devices, body(): lax.all_to_all(jnp.tile(normalized_input, repeats), 'adapter', split_axis...  233 us
    all_to_all x1, starting transfers between devices, body(): lax.all_to_all(jnp.tile(normalized_input, repeats), 'adapter', split_axis...  17 us
  transfers between devices with their start and end apart: 3, of which 3 were waited for; matrix products, arithmetic and copies ran while one was open for 0% of the time, Pallas kernels for 0%

profile of v1, /device:TPU:6, one launch (start us, length us, event | category | flops | bytes accessed | tf_op | source)
XLA Modules:
  0.0 622.0 jit_solution(16064373959628131548)
XLA Ops:
  0.0 0.0 copy-start
  0.0 0.0 collective-permute-start
  0.0 4.6 collective-permute-done
  4.6 0.2 fusion.17
  4.8 0.9 fusion.19
  5.7 4.2 tile.2
  9.9 0.0 copy-start.4
  9.9 0.0 copy-start.2
  9.9 17.0 %all-to-all-start = ((bf16[64,8,8192]{2,1,0:T(8,128)(2,1)}), bf16[64,8,8192]{2,1,0:T(8,128)(2,1)}, u32[]{:S(2)}, u32[]{:S(2)}) async-start(bf16[64,8,8192]{2,1,0:T(8,128)(2,1)} %tile.2), calls=%async_computation | async-start | bytes 16777216 | tf_op jit(solution)/shard_map/all_to_all | solution.py:49
  26.9 0.0 copy-done.4
  26.9 233.1 %all-to-all-done = bf16[64,8,8192]{2,1,0:T(8,128)(2,1)} async-done(((bf16[64,8,8192]{2,1,0:T(8,128)(2,1)}), bf16[64,8,8192]{2,1,0:T(8,128)(2,1)}, u32[]{:S(2)}, u32[]{:S(2)}) %all-to-all-start) | async-done | bytes 8388640 | tf_op jit(solution)/shard_map/all_to_all | solution.py:49
  260.0 0.0 copy-done.2
  260.0 6.0 fusion.13
  266.1 326.1 %all-reduce.1 = bf16[512,64]{0,1:T(8,128)(2,1)S(1)} all-reduce(f32[512,64]{0,1:T(8,128)S(1)} %fusion.13), channel_id=1, replica_groups=mesh['segment'=8,'adapter'=64] {'adapter'}, use_global_device_ids=true, to_apply=%region_1.2 | all-reduce | flops 32768 | bytes 196608 | tf_op jit(solution)/shard_map/psum | solution.py:63
  592.2 0.3 broadcast_multiply_fusion
  592.5 0.0 copy-done
  592.5 0.0 copy-start.1
  592.5 5.8 fusion.3
  598.3 0.0 copy-start.3
  598.3 0.0 copy-done.1
  598.3 2.0 fusion.12
  600.3 6.8 %all-to-all-start.1 = ((bf16[64,8,128]{2,1,0:T(8,128)(2,1)}), bf16[64,8,128]{2,1,0:T(8,128)(2,1)S(1)}, u32[]{:S(2)}, u32[]{:S(2)}) async-start(bf16[64,8,128]{2,1,0:T(8,128)(2,1)} %fusion.12), calls=%async_computation.1 | async-start | bytes 262144 | tf_op jit(solution)/shard_map/all_to_all | solution.py:76
  607.1 0.0 copy-done.3
  607.2 0.8 dynamic_slice.3
  608.0 0.1 iota_compare_fusion.1
  608.1 11.7 %all-to-all-done.1 = bf16[64,8,128]{2,1,0:T(8,128)(2,1)S(1)} async-done(((bf16[64,8,128]{2,1,0:T(8,128)(2,1)}), bf16[64,8,128]{2,1,0:T(8,128)(2,1)S(1)}, u32[]{:S(2)}, u32[]{:S(2)}) %all-to-all-start.1) | async-done | bytes 131104 | tf_op jit(solution)/shard_map/all_to_all | solution.py:76
  619.8 0.3 fusion.7
  620.0 0.2 fusion.27
  620.2 1.0 fusion.11
  621.2 0.7 copy.26
  (6 shorter events, 0.2 us)
Async XLA Ops:
  0.0 592.5 %copy-start = (bf16[1,8192,128]{2,1,0:T(8,128)(2,1)S(1)}, bf16[1,8192,128]{2,1,0:T(8,128)(2,1)}, u32[]{:S(2)}) copy-start(bf16[1,8192,128]{2,1,0:T(8,128)(2,1)} %param.10) | copy-start | bytes 6291460
  0.0 4.6 collective-permute-start
  9.9 17.0 %copy-start.4 = (s32[512]{0:T(512)S(1)}, s32[512]{0:T(512)}, u32[]{:S(2)}) copy-start(s32[512]{0:T(512)} %param.13) | copy-start | bytes 6148
  9.9 250.2 %copy-start.2 = (bf16[1,1,8192,64]{2,3,1,0:T(8,128)(2,1)S(1)}, bf16[1,1,8192,64]{2,3,1,0:T(8,128)(2,1)}, u32[]{:S(2)}) copy-start(bf16[1,1,8192,64]{2,3,1,0:T(8,128)(2,1)} %param.11) | copy-start | bytes 3145732
  9.9 250.2 %all-to-all-start = ((bf16[64,8,8192]{2,1,0:T(8,128)(2,1)}), bf16[64,8,8192]{2,1,0:T(8,128)(2,1)}, u32[]{:S(2)}, u32[]{:S(2)}) async-start(bf16[64,8,8192]{2,1,0:T(8,128)(2,1)} %tile.2), calls=%async_computation | async-start | bytes 16777216 | tf_op jit(solution)/shard_map/all_to_all | solution.py:49
  592.5 5.8 copy-start.1
  598.3 8.8 %copy-start.3 = (bf16[8,2,16,1024]{3,2,1,0:T(8,128)(2,1)S(1)}, bf16[8,2,16,1024]{3,2,1,0:T(8,128)(2,1)}, u32[]{:S(2)}) copy-start(bf16[8,2,16,1024]{3,2,1,0:T(8,128)(2,1)} %param.15) | copy-start | bytes 1572868
  600.3 19.5 %all-to-all-start.1 = ((bf16[64,8,128]{2,1,0:T(8,128)(2,1)}), bf16[64,8,128]{2,1,0:T(8,128)(2,1)S(1)}, u32[]{:S(2)}, u32[]{:S(2)}) async-start(bf16[64,8,128]{2,1,0:T(8,128)(2,1)} %fusion.12), calls=%async_computation.1 | async-start | bytes 262144 | tf_op jit(solution)/shard_map/all_to_all | solution.py:76

commit v2 on v0

--- a/solution.py
+++ b/solution.py
@@ -56,7 +56,7 @@
         owner_of == position
     )[:, None]
     shrunk_mine = jnp.sum(shrunk_all * select_mask[:, :, None].astype(jnp.float32), axis=1)
-    shrunk_tok = lax.psum(shrunk_mine, "adapter").astype(jnp.bfloat16)
+    shrunk_tok = jnp.sum(lax.all_gather(shrunk_mine, "adapter"), axis=0).astype(jnp.bfloat16)
     adapter_hot = (
         request_adapter_index[:, None] == jnp.arange(adapter_bank, dtype=jnp.int32)[None, :]
     ).astype(jnp.bfloat16)

time: 437 us -> 268 us (0.61)
  blocking collectives: 278 us -> 0 us
  waiting for transfers between devices: 119 us -> 212 us
  local copies, waits for them, and re-layouts: 1.66 us -> 10.7 us
    psum x1 -> x0, blocking collectives: 278 us -> none  [body(): shrunk_tok = lax.psum(shrunk_mine, 'adapter').astype(jnp.bfloat16)]
    all_gather x0 -> x1, waiting for transfers between devices: none -> 91.8 us  [body(): lax.all_gather(shrunk_mine, 'adapter')]
    unnamed x9 -> x12, local copies, waits for them, and re-layouts: 0.86 us -> 9.89 us
  transfers between devices with their start and end apart: 3 -> 4, of which waited for: 3 -> 4; matrix products, arithmetic and copies ran while one was open for 1% -> 3% of each run, Pallas kernels for 0% -> 0%
where the time goes in v2:
time: 268 us; the launch traced here: 267 us
  waiting for transfers between devices  212 us (79%)
  matrix products  15.8 us (6%)
  between operations  13.5 us (5%)
  local copies, waits for them, and re-layouts  10.7 us (4%)
  starting transfers between devices  10.1 us (4%)
  other arithmetic  5.58 us (2%)
    all_gather x1, waiting for transfers between devices, body(): row_piece = lax.all_gather(normalized_input, 'adapter', axis=0, tiled=True)  103 us
    all_gather x1, waiting for transfers between devices, body(): lax.all_gather(shrunk_mine, 'adapter')  91.8 us
    all_to_all x1, waiting for transfers between devices, body(): lax.all_to_all(query_rows, 'adapter', split_axis=0, concat_axis=1, tiled=...  11.7 us
    all_to_all x1, starting transfers between devices, body(): lax.all_to_all(query_rows, 'adapter', split_axis=0, concat_axis=1, tiled=...  10 us
    unnamed x12, local copies, waits for them, and re-layouts  9.89 us
    dot_general x1, matrix products, body(): jnp.einsum('td,adr->tar', row_piece, down_matrices, preferred_element_typ...  6.93 us
    dot_general x1, matrix products, body(): plain = jnp.dot(row_piece, weight, preferred_element_type=jnp.float32)  5.7 us
  transfers between devices with their start and end apart: 4, of which 4 were waited for; matrix products, arithmetic and copies ran while one was open for 3% of the time, Pallas kernels for 0%

profile of v2, /device:TPU:2, one launch (start us, length us, event | category | flops | bytes accessed | tf_op | source)
XLA Modules:
  0.0 267.3 jit_solution(282248917349415748)
XLA Ops:
  6.5 0.0 copy-start
  6.5 0.0 all-gather.4.cloned.1.call-start
  6.5 0.0 collective-permute-start
  6.5 4.6 %collective-permute-done = bf16[8,8192]{1,0:T(8,128)(2,1)S(1)} collective-permute-done((bf16[8,8192]{1,0:T(8,128)(2,1)}, bf16[8,8192]{1,0:T(8,128)(2,1)S(1)}, u32[]{:S(2)}, u32[]{:S(2)}) %collective-permute-start) | collective-permute-done | bytes 131104 | tf_op jit(solution)/shard_map/ppermute | solution.py:17
  11.1 0.2 fusion.11
  11.3 1.5 fusion.13
  12.8 0.0 all-gather.4.cloned.1.call-update
  12.9 0.0 all-gather.6.cloned.1.call-start
  12.9 0.7 compare_convert_fusion
  13.6 0.0 copy-start.3
  13.6 103.4 %all-gather.4.cloned.1.call-done = bf16[512,8192]{1,0:T(8,128)(2,1)} async-done(((bf16[8,8192]{1,0:T(8,128)(2,1)}), bf16[512,8192]{1,0:T(8,128)(2,1)}) %all-gather.4.cloned.1.call-update) | async-done | bytes 8388624 | tf_op jit(solution)/shard_map/all_gather | solution.py:47
  117.0 6.9 %convolution_multiply_fusion.2 = f32[512,64]{0,1:T(8,128)} fusion(bf16[512,8192]{1,0:T(8,128)(2,1)} %all-gather.4.cloned.1.call-done, bf16[1,1,8192,64]{2,3,1,0:T(8,128)(2,1)} %param.11, f32[512]{0:T(512)S(1)} %compare_convert_fusion), kind=kOutput, calls=%fused_computation.15 | convolution fusion | flops 536903680 | bytes 9570304 | tf_op jit(solution)/shard_map/td,adr->tar/dot_general | solution.py:49
  124.0 0.0 all-gather.6.cloned.1.call-update
  124.0 0.0 copy-done.3
  124.0 0.0 copy-done
  124.0 5.7 %fusion.1 = f32[512,128]{1,0:T(8,128)S(1)} fusion(bf16[512,8192]{1,0:T(8,128)(2,1)} %all-gather.4.cloned.1.call-done, bf16[1,8192,128]{2,1,0:T(8,128)(2,1)S(1)} %copy-done), kind=kOutput, calls=%fused_computation.2 | convolution fusion | flops 1073741824 | bytes 10747904 | tf_op jit(solution)/shard_map/dot_general | solution.py:48
  129.7 91.8 %all-gather.6.cloned.1.call-done = f32[32768,64]{0,1:T(8,128)} async-done(((f32[512,64]{0,1:T(8,128)}), f32[32768,64]{0,1:T(8,128)}) %all-gather.6.cloned.1.call-update) | async-done | bytes 8388624 | tf_op jit(solution)/shard_map/all_gather | solution.py:59
  221.6 8.1 %copy.13 = f32[8,8,64,512]{3,2,1,0:T(8,128)S(1)} copy(f32[8,8,64,512]{3,1,2,0:T(8,128)} %bitcast.43) | data formatting | bytes 16777216
  229.7 2.6 bitcast_reduce_fusion
  232.3 0.0 copy-start.1
  232.3 0.0 copy-start.2
  232.3 0.3 broadcast_multiply_fusion
  232.6 0.9 copy-done.1
  233.5 2.0 fusion.9
  235.5 10.0 %all-to-all-start = ((bf16[64,8,128]{2,1,0:T(8,128)(2,1)}), bf16[64,8,128]{2,1,0:T(8,128)(2,1)S(1)}, u32[]{:S(2)}, u32[]{:S(2)}) async-start(bf16[64,8,128]{2,1,0:T(8,128)(2,1)} %fusion.9), calls=%async_computation | async-start | bytes 262144 | tf_op jit(solution)/shard_map/all_to_all | solution.py:72
  245.5 0.0 copy-done.2
  245.7 0.8 dynamic_slice.3
  246.4 0.1 iota_compare_fusion.1
  246.5 11.7 %all-to-all-done = bf16[64,8,128]{2,1,0:T(8,128)(2,1)S(1)} async-done(((bf16[64,8,128]{2,1,0:T(8,128)(2,1)}), bf16[64,8,128]{2,1,0:T(8,128)(2,1)S(1)}, u32[]{:S(2)}, u32[]{:S(2)}) %all-to-all-start) | async-done | bytes 131104 | tf_op jit(solution)/shard_map/all_to_all | solution.py:72
  258.2 0.3 fusion.4
  258.5 0.2 fusion.21
  258.7 1.0 fusion.8
  259.7 0.7 copy.26
  (5 shorter events, 0.2 us)
Async XLA Ops:
  6.5 117.5 %copy-start = (bf16[1,8192,128]{2,1,0:T(8,128)(2,1)S(1)}, bf16[1,8192,128]{2,1,0:T(8,128)(2,1)}, u32[]{:S(2)}) copy-start(bf16[1,8192,128]{2,1,0:T(8,128)(2,1)} %param.10) | copy-start | bytes 6291460
  6.5 110.5 %all-gather.4.cloned.1.call-start = ((), (), s32[]{:S(2)}) async-start(), calls=%async_computation.1 | async-start | bytes 8519680 | tf_op jit(solution)/shard_map/all_gather | solution.py:47
  6.5 4.6 %collective-permute-start = (bf16[8,8192]{1,0:T(8,128)(2,1)}, bf16[8,8192]{1,0:T(8,128)(2,1)S(1)}, u32[]{:S(2)}, u32[]{:S(2)}) collective-permute-start(bf16[8,8192]{1,0:T(8,128)(2,1)} %param.8), channel_id=1, source_target_pairs={{0,64},{64,128},{128,192},{192,256},{256,320},{320,384},{384,448},... | collective-permute-start | bytes 393224 | tf_op jit(solution)/shard_map/ppermute | solution.py:17
  12.9 208.7 %all-gather.6.cloned.1.call-start = ((), (), s32[]{:S(2)}) async-start(), calls=%async_computation.2 | async-start | bytes 8519680 | tf_op jit(solution)/shard_map/all_gather | solution.py:59
  13.6 110.4 %copy-start.3 = (s32[512]{0:T(512)S(1)}, s32[512]{0:T(512)}, u32[]{:S(2)}) copy-start(s32[512]{0:T(512)} %param.13) | copy-start | bytes 6148
  232.3 1.2 copy-start.1
  232.3 13.2 %copy-start.2 = (bf16[8,2,16,1024]{3,2,1,0:T(8,128)(2,1)S(1)}, bf16[8,2,16,1024]{3,2,1,0:T(8,128)(2,1)}, u32[]{:S(2)}) copy-start(bf16[8,2,16,1024]{3,2,1,0:T(8,128)(2,1)} %param.15) | copy-start | bytes 1572868
  235.5 22.8 %all-to-all-start = ((bf16[64,8,128]{2,1,0:T(8,128)(2,1)}), bf16[64,8,128]{2,1,0:T(8,128)(2,1)S(1)}, u32[]{:S(2)}, u32[]{:S(2)}) async-start(bf16[64,8,128]{2,1,0:T(8,128)(2,1)} %fusion.9), calls=%async_computation | async-start | bytes 262144 | tf_op jit(solution)/shard_map/all_to_all | solution.py:72
Sparse Core Ops, SparseCore 0:
  13.0 103.9 all-gather.3
  124.1 97.4 all-gather.5
